TPU v7x, 32 devices: a whole 2x2x4 slice. The times are simulated.
32 devices in a mesh: roll: 4 (over y, x), seq: 8 (over z, core).
Axes of the slice: x: 2, y: 2, z: 4, core: 2. Of those that a mesh axis runs over, the one named last changes fastest.
Arguments:
- query_rows: bfloat16 [4, 4096, 1792], P('roll', 'seq'), may hold values from -200 to 200
- key_rows: bfloat16 [4, 4096, 256], P('roll', 'seq'), may hold values from -6 to 6
- value_rows: bfloat16 [4, 4096, 256], P('roll', 'seq'), may hold values from -6 to 6
- cotangent: bfloat16 [4, 4096, 1792], P('roll', None, 'seq'), may hold values from -6 to 6
- slopes: float32 [14], replicated, may hold values from 0.00029296876 to 0.0390625
- lengths: int32 [4], P('roll'), may hold values from 1024 to 4096, as said below
- loss_mask: int32 [4, 4096], P('roll', 'seq'), may hold values 0 or 1
- distances: int32 [4], P('roll'), may hold values from 40 to 357
Outputs:
- grad_queries: bfloat16 [4, 4096, 1792], P('roll', 'seq')
- grad_keys: bfloat16 [4, 4096, 256], P('roll', 'seq')
- grad_values: bfloat16 [4, 4096, 256], P('roll', 'seq')
Inputs may be any that keep to these rules, and one draw needn't show every extreme that they name: `lengths`: some rollout has 4096 tokens and some 4096 // 4.
All inputs are finite; a program needn't handle non-finite values. No bound on the sum of `loss_mask` on one device may be relied on, other than what follows from the above.
Results may differ from a plain program's by a relative error of at most 0.0068.
Values may be sent and summed in bfloat16 or wider, within the bound.
No kernel may reach another device: no remote copies, remote signals or barrier semaphores. Data moves between devices by JAX's collectives and lax.ppermute only.
A program may use at most 64 MiB of HBM per device.

v0:
```python
import math
import jax
import jax.numpy as jnp
from jax import lax
from jax.sharding import PartitionSpec as P

HEAD_DIM = 128
WINDOW = 1024


def passed_along(value, axis, steps):
    count = lax.axis_size(axis)
    leading, last = (max(0, -steps), min(count, count - steps))
    return lax.ppermute(value, axis, [(source, source + steps) for source in range(leading, last)])


def shards(query_rows, key_rows, value_rows, cotangent, slopes, lengths, loss_mask, distances):
    own_q = query_rows[0]
    own_k = key_rows[0]
    own_v = value_rows[0]
    tok_rows = own_q.shape[0]
    features = own_q.shape[1]
    kv_features = own_k.shape[1]
    head_dim = HEAD_DIM
    head_count = features // head_dim
    kv_count = kv_features // head_dim
    group_size = head_count // kv_count
    band_reach = (WINDOW - 2) // tok_rows + 1
    band_len = (band_reach + 1) * tok_rows
    seq_len = tok_rows * lax.axis_size("seq")
    seq_pos = lax.axis_index("seq")
    attn_scale = 1.0 / math.sqrt(head_dim)
    positions = seq_pos * tok_rows + jnp.arange(tok_rows, dtype=jnp.int32)
    valid = ((positions < lengths[0]) & (loss_mask[0] == 1)).astype(jnp.float32)
    local_count = jnp.sum(valid)
    my_distance = distances[0].astype(jnp.float32)
    count_all = lax.psum(local_count, "seq")
    group_total = lax.psum(my_distance, "roll")
    advantage = (group_total / lax.axis_size("roll") - my_distance) / 64.0
    weight = advantage * valid * seq_len / (1.0 + count_all)
    arrived = lax.all_to_all(cotangent, "seq", split_axis=1, concat_axis=2, tiled=True)[0]
    dout = (arrived.astype(jnp.float32) * weight[:, None]).astype(jnp.bfloat16)
    kv_pair = jnp.stack([own_k, own_v])
    earlier = []
    for offset in range(1, band_reach + 1):
        earlier.append(passed_along(kv_pair, "seq", offset))
    ordered = earlier[::-1]
    band_k = jnp.concatenate([blk[0] for blk in ordered] + [own_k], 0)
    band_v = jnp.concatenate([blk[1] for blk in ordered] + [own_v], 0)
    key_pos = (seq_pos - band_reach) * tok_rows + jnp.arange(band_len, dtype=jnp.int32)
    pos_gap = positions[:, None] - key_pos[None, :]
    allowed = (pos_gap >= 0) & (pos_gap < WINDOW) & (key_pos[None, :] >= 0)
    gap_float = pos_gap.astype(jnp.float32)
    split_at = band_reach * tok_rows
    contract_rows = (((0,), (0,)), ((), ()))

    def head_step(head, carry):
        grad_q, own_dk, own_dv, part_k, part_v = carry
        column = head * head_dim
        kv_column = head // group_size * head_dim
        q_head = lax.dynamic_slice_in_dim(own_q, column, head_dim, 1)
        k_head = lax.dynamic_slice_in_dim(band_k, kv_column, head_dim, 1)
        v_head = lax.dynamic_slice_in_dim(band_v, kv_column, head_dim, 1)
        d_head = lax.dynamic_slice_in_dim(dout, column, head_dim, 1)
        slope = lax.dynamic_index_in_dim(slopes, head, keepdims=False)
        scores = (
            jnp.dot(q_head, k_head.T, preferred_element_type=jnp.float32) * attn_scale
            - slope * gap_float
        )
        masked = jnp.where(allowed, scores, -jnp.inf)
        row_max = jnp.max(masked, axis=1, keepdims=True)
        exp_terms = jnp.where(allowed, jnp.exp(masked - row_max), 0.0)
        probs = exp_terms / jnp.sum(exp_terms, axis=1, keepdims=True)
        probs_low = probs.astype(jnp.bfloat16)
        dprob = jnp.dot(d_head, v_head.T, preferred_element_type=jnp.float32)
        row_delta = jnp.sum(probs * dprob, axis=1, keepdims=True)
        dscore = (probs * (dprob - row_delta) * attn_scale).astype(jnp.bfloat16)
        head_dq = jnp.dot(dscore, k_head, preferred_element_type=jnp.float32).astype(jnp.bfloat16)
        band_dk = lax.dot_general(dscore, q_head, contract_rows, preferred_element_type=jnp.float32)
        band_dv = lax.dot_general(
            probs_low, d_head, contract_rows, preferred_element_type=jnp.float32
        )
        grad_q = lax.dynamic_update_slice_in_dim(grad_q, head_dq, column, 1)
        own_dk = lax.dynamic_update_slice_in_dim(
            own_dk,
            lax.dynamic_slice_in_dim(own_dk, kv_column, head_dim, 1) + band_dk[split_at:],
            kv_column,
            1,
        )
        own_dv = lax.dynamic_update_slice_in_dim(
            own_dv,
            lax.dynamic_slice_in_dim(own_dv, kv_column, head_dim, 1) + band_dv[split_at:],
            kv_column,
            1,
        )
        far_dk = band_dk[:split_at].reshape(band_reach, tok_rows, head_dim)
        far_dv = band_dv[:split_at].reshape(band_reach, tok_rows, head_dim)
        part_k = lax.dynamic_update_slice_in_dim(
            part_k, lax.dynamic_slice_in_dim(part_k, kv_column, head_dim, 2) + far_dk, kv_column, 2
        )
        part_v = lax.dynamic_update_slice_in_dim(
            part_v, lax.dynamic_slice_in_dim(part_v, kv_column, head_dim, 2) + far_dv, kv_column, 2
        )
        return (grad_q, own_dk, own_dv, part_k, part_v)

    start_carry = (
        jnp.zeros((tok_rows, features), jnp.bfloat16),
        jnp.zeros((tok_rows, kv_features), jnp.float32),
        jnp.zeros((tok_rows, kv_features), jnp.float32),
        jnp.zeros((band_reach, tok_rows, kv_features), jnp.float32),
        jnp.zeros((band_reach, tok_rows, kv_features), jnp.float32),
    )
    grad_q, total_k, total_v, part_k, part_v = lax.fori_loop(0, head_count, head_step, start_carry)
    part_k = part_k.astype(jnp.bfloat16)
    part_v = part_v.astype(jnp.bfloat16)
    for offset in range(1, band_reach + 1):
        outgoing = jnp.stack([part_k[band_reach - offset], part_v[band_reach - offset]])
        incoming = passed_along(outgoing, "seq", -offset)
        total_k = total_k + incoming[0].astype(jnp.float32)
        total_v = total_v + incoming[1].astype(jnp.float32)
    return (grad_q[None], total_k.astype(jnp.bfloat16)[None], total_v.astype(jnp.bfloat16)[None])


def solution(mesh):
    placed = (
        P("roll", "seq", None),
        P("roll", "seq", None),
        P("roll", "seq", None),
        P("roll", None, "seq"),
        P(),
        P("roll"),
        P("roll", "seq"),
        P("roll"),
    )
    return jax.shard_map(
        shards,
        mesh=mesh,
        in_specs=placed,
        out_specs=(P("roll", "seq", None), P("roll", "seq", None), P("roll", "seq", None)),
        check_vma=False,
    )
```

profile of v0, /device:TPU:19, one launch (start us, length us, event | category | flops | bytes accessed | tf_op | source)
XLA Modules:
  0.0 346.7 jit_solution(13123298232539514425)
XLA Ops:
  0.6 10.0 %copy.19 = bf16[1,4096,224]{2,0,1:T(2,128)(2,1)} copy(bf16[1,4096,224]{1,2,0:T(8,128)(2,1)} %param.13) | data formatting | bytes 3670016 | tf_op args[3]
  11.1 23.6 %reduce.2 = bf16[4096,224]{1,0:T(8,128)(2,1)S(1)} reduce(bf16[4096,1,224]{2,1,0:T(2,128)(2,1)} %bitcast.71, bf16[]{:T(256)} %broadcast.76), dimensions={1}, to_apply=%bitcast.53.reduce_sub_computation | reduce | bytes 3670018
  34.8 5.2 %reshape.80 = bf16[8,2,57344]{2,1,0:T(2,128)(2,1)} reshape(bf16[4096,224]{1,0:T(8,128)(2,1)S(1)} %reduce.2) | data formatting | bytes 3670016
  40.0 5.7 %all-to-all-start = ((bf16[8,2,57344]{2,1,0:T(2,128)(2,1)}), bf16[8,2,57344]{2,1,0:T(2,128)(2,1)S(1)}, u32[]{:S(2)}, u32[]{:S(2)}) async-start(bf16[8,2,57344]{2,1,0:T(2,128)(2,1)} %reshape.80), calls=%async_computation | async-start | bytes 3670016 | tf_op jit(solution)/shard_map/all_to_all | solution.py:41
  47.1 3.3 collective-permute-start.1
  50.4 1.9 collective-permute-start
  54.3 7.8 %psum.14 = f32[]{:T(128)} all-reduce(f32[]{:T(128)} %bitcast.7), channel_id=1, replica_groups=mesh['roll'=4,'seq'=8] {'roll'}, use_global_device_ids=true, to_apply=%region_0.0 | all-reduce | flops 1 | bytes 8 | tf_op jit(solution)/shard_map/psum | solution.py:38
  62.0 47.4 %psum.15 = f32[]{:T(128)} all-reduce(f32[]{:T(128)} %convert_reduce_fusion), channel_id=1, replica_groups=mesh['roll'=4,'seq'=8] {'seq'}, use_global_device_ids=true, to_apply=%region_2.0 | all-reduce | flops 1 | bytes 8 | tf_op jit(solution)/shard_map/psum | solution.py:37
  113.1 5.8 %reshape.81 = bf16[4096,1,224]{2,1,0:T(2,128)(2,1)} reshape(bf16[8,2,57344]{2,1,0:T(2,128)(2,1)S(1)} %all-to-all-done) | data formatting | bytes 3670016
  118.9 10.1 %copy.20 = bf16[1,4096,224]{1,2,0:T(8,128)(2,1)S(1)} copy(bf16[1,4096,224]{2,0,1:T(2,128)(2,1)} %bitcast.72) | data formatting | bytes 3670016 | tf_op jit(solution)/shard_map/all_to_all | solution.py:41
  129.5 3.3 copy.24
  132.7 2.1 copy.21
  134.9 1.8 fusion.30
  138.3 186.0 %while.25 = (s32[]{:T(128)}, bf16[512,1792]{1,0:T(8,128)(2,1)}, f32[512,256]{1,0:T(8,128)S(1)}, f32[512,256]{1,0:T(8,128)S(1)}, f32[2,512,256]{2,1,0:T(8,128)S(1...) while((s32[]{:T(128)}, bf16[512,1792]{1,0:T(8,128)(2,1)}, ...), condition=%wide.region_7.8_spmd.clone.clone, body=%wide.region_3.7_spmd.clone.clone.sunk | while | flops 1033828864 | bytes 46446556 | solution.py:113
  138.8 3.3 fusion.59
  143.5 2.8 multiply_reduce_fusion.2
  152.1 3.3 fusion.59
  156.8 2.8 multiply_reduce_fusion.2
  165.4 3.3 fusion.59
  170.0 2.8 multiply_reduce_fusion.2
  178.6 3.3 fusion.59
  183.3 2.8 multiply_reduce_fusion.2
  191.9 3.3 fusion.59
  196.6 2.8 multiply_reduce_fusion.2
  205.2 3.3 fusion.59
  209.8 2.8 multiply_reduce_fusion.2
  218.4 3.3 fusion.59
  223.1 2.8 multiply_reduce_fusion.2
  231.7 3.3 fusion.59
  236.3 2.8 multiply_reduce_fusion.2
  239.6 1.6 fusion.62
  245.0 3.3 fusion.59
  249.7 2.8 multiply_reduce_fusion.2
  252.9 1.6 fusion.62
  258.3 3.3 fusion.59
  263.0 2.8 multiply_reduce_fusion.2
  271.7 3.3 fusion.59
  276.3 2.8 multiply_reduce_fusion.2
  285.0 3.3 fusion.59
  289.6 2.8 multiply_reduce_fusion.2
  298.3 3.3 fusion.59
  303.0 2.8 multiply_reduce_fusion.2
  311.6 3.3 fusion.59
  316.3 2.8 multiply_reduce_fusion.2
  324.6 1.9 collective-permute-start.3
  326.6 2.1 collective-permute-start.2
  328.7 11.2 %collective-permute-done.3 = bf16[2,512,256]{2,1,0:T(8,128)(2,1)S(1)} collective-permute-done((bf16[2,512,256]{2,1,0:T(8,128)(2,1)S(1)}, bf16[2,512,256]{2,1,0:T(8,128)(2,1)S(1)}, u32[]{:S(2)}, u32[]{:S(2)}) %collective-permute-start.3) | collective-permute-done | bytes 524320 | tf_op jit(solution)/shard_map/ppermute | solution.py:14
  339.9 5.9 %collective-permute-done.2 = bf16[2,512,256]{2,1,0:T(8,128)(2,1)S(1)} collective-permute-done((bf16[2,512,256]{2,1,0:T(8,128)(2,1)S(1)}, bf16[2,512,256]{2,1,0:T(8,128)(2,1)S(1)}, u32[]{:S(2)}, u32[]{:S(2)}) %collective-permute-start.2) | collective-permute-done | bytes 524320 | tf_op jit(solution)/shard_map/ppermute | solution.py:14
  (230 shorter events, 104.8 us)
Async XLA Ops:
  34.7 10.9 %copy-start.1 = (bf16[1,512,256]{2,1,0:T(8,128)(2,1)S(1)}, bf16[1,512,256]{2,1,0:T(8,128)(2,1)}, u32[]{:S(2)}) copy-start(bf16[1,512,256]{2,1,0:T(8,128)(2,1)} %param.11) | copy-start | bytes 786436
  34.8 11.6 %copy-start.2 = (bf16[1,512,256]{2,1,0:T(8,128)(2,1)S(1)}, bf16[1,512,256]{2,1,0:T(8,128)(2,1)}, u32[]{:S(2)}) copy-start(bf16[1,512,256]{2,1,0:T(8,128)(2,1)} %param.12) | copy-start | bytes 786436
  40.0 13.7 %copy-start.4 = (s32[1,512]{1,0:T(1,128)S(1)}, s32[1,512]{1,0:T(1,128)}, u32[]{:S(2)}) copy-start(s32[1,512]{1,0:T(1,128)} %param.16) | copy-start | bytes 6148
  40.0 73.2 %all-to-all-start = ((bf16[8,2,57344]{2,1,0:T(2,128)(2,1)}), bf16[8,2,57344]{2,1,0:T(2,128)(2,1)S(1)}, u32[]{:S(2)}, u32[]{:S(2)}) async-start(bf16[8,2,57344]{2,1,0:T(2,128)(2,1)} %reshape.80), calls=%async_computation | async-start | bytes 3670016 | tf_op jit(solution)/shard_map/all_to_all | solution.py:41
  47.1 63.7 %collective-permute-start.1 = (bf16[2,512,256]{2,1,0:T(8,128)(2,1)}, bf16[2,512,256]{2,1,0:T(8,128)(2,1)}, u32[]{:S(2)}, u32[]{:S(2)}) collective-permute-start(bf16[2,512,256]{2,1,0:T(8,128)(2,1)} %constant_dynamic-update-slice_fusion), channel_id=1, source_target_pairs={{0,1},{1,2},{2,3},{3,4},{4,5},{5,6},{6,7},{8,9},{9,10},{10,11},{11... | collective-permute-start | bytes 1572872 | tf_op jit(solution)/shard_map/ppermute | solution.py:14
  50.4 61.4 %collective-permute-start = (bf16[2,512,256]{2,1,0:T(8,128)(2,1)}, bf16[2,512,256]{2,1,0:T(8,128)(2,1)S(1)}, u32[]{:S(2)}, u32[]{:S(2)}) collective-permute-start(bf16[2,512,256]{2,1,0:T(8,128)(2,1)} %constant_dynamic-update-slice_fusion), channel_id=1, source_target_pairs={{0,2},{1,3},{2,4},{3,5},{4,6},{5,7},{8,10},{9,11},{10,12},{11,13},... | collective-permute-start | bytes 1572872 | tf_op jit(solution)/shard_map/ppermute | solution.py:14
  136.7 1.6 copy-start.5
  142.1 1.4 copy-start.3
  146.7 3.2 copy-start
  155.4 1.4 copy-start.3
  160.0 3.2 copy-start
  168.6 1.4 copy-start.3
  173.2 3.2 copy-start
  181.9 1.4 copy-start.3
  186.5 3.2 copy-start
  195.2 1.4 copy-start.3
  199.8 3.2 copy-start
  208.4 1.4 copy-start.3
  213.0 3.2 copy-start
  221.7 1.4 copy-start.3
  226.3 3.2 copy-start
  235.0 1.4 copy-start.3
  239.6 3.2 copy-start
  248.3 1.4 copy-start.3
  252.9 3.2 copy-start
  261.6 1.4 copy-start.3
  266.2 3.2 copy-start
  274.9 1.4 copy-start.3
  279.5 3.2 copy-start
  288.3 1.4 copy-start.3
  292.8 3.2 copy-start
  301.6 1.4 copy-start.3
  306.2 3.2 copy-start
  314.9 1.4 copy-start.3
  319.5 3.2 copy-start
  324.6 15.3 %collective-permute-start.3 = (bf16[2,512,256]{2,1,0:T(8,128)(2,1)S(1)}, bf16[2,512,256]{2,1,0:T(8,128)(2,1)S(1)}, u32[]{:S(2)}, u32[]{:S(2)}) collective-permute-start(bf16[2,512,256]{2,1,0:T(8,128)(2,1)S(1)} %pad_maximum_fusion.3), channel_id=1, source_target_pairs={{2,0},{3,1},{4,2},{5,3},{6,4},{7,5},{10,8},{11,9},{12,10},{13,11},... | collective-permute-start | bytes 1572872 | tf_op jit(solution)/shard_map/ppermute | solution.py:14
  326.6 19.2 %collective-permute-start.2 = (bf16[2,512,256]{2,1,0:T(8,128)(2,1)S(1)}, bf16[2,512,256]{2,1,0:T(8,128)(2,1)S(1)}, u32[]{:S(2)}, u32[]{:S(2)}) collective-permute-start(bf16[2,512,256]{2,1,0:T(8,128)(2,1)S(1)} %pad_maximum_fusion.2), channel_id=1, source_target_pairs={{1,0},{2,1},{3,2},{4,3},{5,4},{6,5},{7,6},{9,8},{10,9},{11,10},{12... | collective-permute-start | bytes 1572872 | tf_op jit(solution)/shard_map/ppermute | solution.py:14
where the time goes:
time: 349 us; the launch traced here: 347 us
  matrix products  146 us (42%)
  other arithmetic  58.4 us (17%)
  blocking collectives  55.2 us (16%)
  local copies, waits for them, and re-layouts  50.5 us (14%)
  waiting for transfers between devices  17.1 us (5%)
  starting transfers between devices  14.9 us (4%)
    psum x1, blocking collectives, shards(): count_all = lax.psum(local_count, 'seq')  47.4 us
    dot_general x14, matrix products, head_step(): jnp.dot(q_head, k_head.T, preferred_element_type=jnp.float32) * attn_scale  45.8 us
    dot_general x14, matrix products, head_step(): dprob = jnp.dot(d_head, v_head.T, preferred_element_type=jnp.float32)  38.8 us
    unnamed x14, local copies, waits for them, and re-layouts  25.4 us
    unnamed x1, other arithmetic  23.6 us
    dot_general x14, matrix products, head_step(): lax.dot_general(probs_low, d_head, contract_rows, preferred_element_type=...  22.3 us
    dot_general x14, matrix products, head_step(): lax.dot_general(dscore, q_head, contract_rows, preferred_element_type=jnp...  21.3 us
    reduce_sum x14, other arithmetic, head_step(): probs = exp_terms / jnp.sum(exp_terms, axis=1, keepdims=True)  19.1 us
  transfers between devices with their start and end apart: 5, of which 2 were waited for; matrix products, arithmetic and copies ran while one was open for 1% of the time, Pallas kernels for 0%

commit v1 on v0

--- a/solution.py
+++ b/solution.py
@@ -6,6 +6,13 @@
 
 HEAD_DIM = 128
 WINDOW = 1024
+
+
+def exchange_blocks(value, axis, split, join):
+    size = lax.axis_size(axis)
+    blocks = jnp.stack(jnp.split(value, size, axis=split), axis=0)
+    blocks = lax.all_to_all(blocks, axis, split_axis=0, concat_axis=0)
+    return jnp.concatenate(blocks, axis=join)
 
 
 def passed_along(value, axis, steps):
@@ -38,7 +45,7 @@
     group_total = lax.psum(my_distance, "roll")
     advantage = (group_total / lax.axis_size("roll") - my_distance) / 64.0
     weight = advantage * valid * seq_len / (1.0 + count_all)
-    arrived = lax.all_to_all(cotangent, "seq", split_axis=1, concat_axis=2, tiled=True)[0]
+    arrived = exchange_blocks(cotangent, "seq", 1, 2)[0]
     dout = (arrived.astype(jnp.float32) * weight[:, None]).astype(jnp.bfloat16)
     kv_pair = jnp.stack([own_k, own_v])
     earlier = []

time: 349 us -> 300 us (0.86)
  local copies, waits for them, and re-layouts: 50.5 us -> 25.6 us
  other arithmetic: 58.4 us -> 34.8 us
    unnamed x1 -> x0, other arithmetic: 23.6 us -> none
    unnamed x14 -> x16, local copies, waits for them, and re-layouts: 25.4 us -> 12.2 us
    all_to_all x1 -> x0, local copies, waits for them, and re-layouts: 10.1 us -> none  [shards(): lax.all_to_all(cotangent, 'seq', split_axis=1, concat_axis=2, tiled=True)[0]]
where the time goes in v1:
time: 300 us; the launch traced here: 298 us
  matrix products  146 us (49%)
  blocking collectives  55.2 us (18%)
  other arithmetic  34.8 us (12%)
  local copies, waits for them, and re-layouts  25.6 us (9%)
  waiting for transfers between devices  17.1 us (6%)
  starting transfers between devices  14.9 us (5%)
  between operations  3.38 us (1%)
    psum x1, blocking collectives, shards(): count_all = lax.psum(local_count, 'seq')  47.4 us
    dot_general x14, matrix products, head_step(): jnp.dot(q_head, k_head.T, preferred_element_type=jnp.float32) * attn_scale  45.8 us
    dot_general x14, matrix products, head_step(): dprob = jnp.dot(d_head, v_head.T, preferred_element_type=jnp.float32)  38.8 us
    dot_general x14, matrix products, head_step(): lax.dot_general(dscore, q_head, contract_rows, preferred_element_type=jnp...  22.2 us
    dot_general x14, matrix products, head_step(): lax.dot_general(probs_low, d_head, contract_rows, preferred_element_type=...  21.3 us
    reduce_sum x14, other arithmetic, head_step(): probs = exp_terms / jnp.sum(exp_terms, axis=1, keepdims=True)  19.1 us
    dot_general x14, matrix products, head_step(): jnp.dot(dscore, k_head, preferred_element_type=jnp.float32)  17.4 us
    ppermute x4, waiting for transfers between devices, passed_along(): lax.ppermute(value, axis, [(source, source + steps) for source in range(l...  17.1 us
  transfers between devices with their start and end apart: 5, of which 2 were waited for; matrix products, arithmetic and copies ran while one was open for 1% of the time, Pallas kernels for 0%

profile of v1, /device:TPU:19, one launch (start us, length us, event | category | flops | bytes accessed | tf_op | source)
XLA Modules:
  0.0 298.2 jit_solution(8794540132780528772)
XLA Ops:
  0.6 1.6 bitcast_dynamic-update-slice_fusion.7
  2.3 1.6 bitcast_dynamic-update-slice_fusion.6
  3.9 1.6 bitcast_dynamic-update-slice_fusion.5
  5.6 1.6 bitcast_dynamic-update-slice_fusion.4
  7.2 1.6 bitcast_dynamic-update-slice_fusion.3
  8.8 1.6 bitcast_dynamic-update-slice_fusion.2
  10.5 1.6 bitcast_dynamic-update-slice_fusion.1
  12.1 1.6 bitcast_dynamic-update-slice_fusion
  13.8 5.7 %all-to-all-start = ((bf16[8,1,512,224]{2,3,1,0:T(8,128)(2,1)}), bf16[8,1,512,224]{2,3,1,0:T(8,128)(2,1)S(1)}, u32[]{:S(2)}, u32[]{:S(2)}) async-start(bf16[8,1,512,224]{2,3,1,0:T(8,128)(2,1)} %bitcast_dynamic-update-slice_fusion), calls=%async_computation | async-start | bytes 3670016 | tf_op jit(solution)/shard_map/all_to_all | solution.py:14
  20.9 3.3 %collective-permute-start.1 = (bf16[2,512,256]{2,1,0:T(8,128)(2,1)}, bf16[2,512,256]{2,1,0:T(8,128)(2,1)S(1)}, u32[]{:S(2)}, u32[]{:S(2)}) collective-permute-start(bf16[2,512,256]{2,1,0:T(8,128)(2,1)} %constant_dynamic-update-slice_fusion), channel_id=1, source_target_pairs={{0,1},{1,2},{2,3},{3,4},{4,5},{5,6},{6,7},{8,9},{9,10},{10,11},{11... | collective-permute-start | bytes 1572872 | tf_op jit(solution)/shard_map/ppermute | solution.py:21
  24.2 1.9 collective-permute-start
  28.1 7.8 %psum.14 = f32[]{:T(128)} all-reduce(f32[]{:T(128)} %bitcast.16), channel_id=1, replica_groups=mesh['roll'=4,'seq'=8] {'roll'}, use_global_device_ids=true, to_apply=%region_0.0 | all-reduce | flops 1 | bytes 8 | tf_op jit(solution)/shard_map/psum | solution.py:45
  35.9 47.4 %psum.15 = f32[]{:T(128)} all-reduce(f32[]{:T(128)} %convert_reduce_fusion), channel_id=1, replica_groups=mesh['roll'=4,'seq'=8] {'seq'}, use_global_device_ids=true, to_apply=%region_2.0 | all-reduce | flops 1 | bytes 8 | tf_op jit(solution)/shard_map/psum | solution.py:44
  86.4 1.8 fusion.30
  89.8 186.0 %while.25 = (s32[]{:T(128)}, bf16[512,1792]{1,0:T(8,128)(2,1)}, f32[512,256]{1,0:T(8,128)S(1)}, f32[512,256]{1,0:T(8,128)S(1)}, f32[2,512,256]{2,1,0:T(8,128)S(1...) while((s32[]{:T(128)}, bf16[512,1792]{1,0:T(8,128)(2,1)}, ...), condition=%wide.region_7.8_spmd.clone.clone, body=%wide.region_3.7_spmd.clone.clone.sunk | while | flops 1033828864 | bytes 46446556 | solution.py:120
  90.4 3.3 %fusion.59 = (f32[512]{0:T(512)S(1)}, f32[512,1536]{1,0:T(8,128)S(1)}) fusion(f32[]{:T(128)} %bitcast.74, bf16[1536,256]{1,0:T(8,128)(2,1)} %get-tuple-element.625, s32[]{:T(128)S(6)} %select_n.97, bf16[512,1792]{1,0:T(8,128)(2,1)} %get-tuple-element.624, s32[]{:T(128)S(6)} %select_n.95, pred[1536]{0:T(1024)(128)(4,1)S(1)} %get-tuple-element.631, ...), kind=kOutput, calls=%fused_computation.80.clone.1 | convolution fusion | flops 209976832 | bytes 3682312 | tf_op jit(solution)/shard_map/while/body/eval_jaxpr/dot_general | solution.py:74
  95.1 2.8 multiply_reduce_fusion.2
  103.7 3.3 %fusion.59 = (f32[512]{0:T(512)S(1)}, f32[512,1536]{1,0:T(8,128)S(1)}) fusion(f32[]{:T(128)} %bitcast.74, bf16[1536,256]{1,0:T(8,128)(2,1)} %get-tuple-element.625, s32[]{:T(128)S(6)} %select_n.97, bf16[512,1792]{1,0:T(8,128)(2,1)} %get-tuple-element.624, s32[]{:T(128)S(6)} %select_n.95, pred[1536]{0:T(1024)(128)(4,1)S(1)} %get-tuple-element.631, ...), kind=kOutput, calls=%fused_computation.80.clone.1 | convolution fusion | flops 209976832 | bytes 3682312 | tf_op jit(solution)/shard_map/while/body/eval_jaxpr/dot_general | solution.py:74
  108.3 2.8 multiply_reduce_fusion.2
  113.1 1.6 fusion.63
  116.9 3.3 %fusion.59 = (f32[512]{0:T(512)S(1)}, f32[512,1536]{1,0:T(8,128)S(1)}) fusion(f32[]{:T(128)} %bitcast.74, bf16[1536,256]{1,0:T(8,128)(2,1)} %get-tuple-element.625, s32[]{:T(128)S(6)} %select_n.97, bf16[512,1792]{1,0:T(8,128)(2,1)} %get-tuple-element.624, s32[]{:T(128)S(6)} %select_n.95, pred[1536]{0:T(1024)(128)(4,1)S(1)} %get-tuple-element.631, ...), kind=kOutput, calls=%fused_computation.80.clone.1 | convolution fusion | flops 209976832 | bytes 3682312 | tf_op jit(solution)/shard_map/while/body/eval_jaxpr/dot_general | solution.py:74
  121.6 2.8 multiply_reduce_fusion.2
  130.2 3.3 %fusion.59 = (f32[512]{0:T(512)S(1)}, f32[512,1536]{1,0:T(8,128)S(1)}) fusion(f32[]{:T(128)} %bitcast.74, bf16[1536,256]{1,0:T(8,128)(2,1)} %get-tuple-element.625, s32[]{:T(128)S(6)} %select_n.97, bf16[512,1792]{1,0:T(8,128)(2,1)} %get-tuple-element.624, s32[]{:T(128)S(6)} %select_n.95, pred[1536]{0:T(1024)(128)(4,1)S(1)} %get-tuple-element.631, ...), kind=kOutput, calls=%fused_computation.80.clone.1 | convolution fusion | flops 209976832 | bytes 3682312 | tf_op jit(solution)/shard_map/while/body/eval_jaxpr/dot_general | solution.py:74
  134.8 2.8 multiply_reduce_fusion.2
  143.4 3.3 %fusion.59 = (f32[512]{0:T(512)S(1)}, f32[512,1536]{1,0:T(8,128)S(1)}) fusion(f32[]{:T(128)} %bitcast.74, bf16[1536,256]{1,0:T(8,128)(2,1)} %get-tuple-element.625, s32[]{:T(128)S(6)} %select_n.97, bf16[512,1792]{1,0:T(8,128)(2,1)} %get-tuple-element.624, s32[]{:T(128)S(6)} %select_n.95, pred[1536]{0:T(1024)(128)(4,1)S(1)} %get-tuple-element.631, ...), kind=kOutput, calls=%fused_computation.80.clone.1 | convolution fusion | flops 209976832 | bytes 3682312 | tf_op jit(solution)/shard_map/while/body/eval_jaxpr/dot_general | solution.py:74
  148.1 2.8 multiply_reduce_fusion.2
  156.7 3.3 %fusion.59 = (f32[512]{0:T(512)S(1)}, f32[512,1536]{1,0:T(8,128)S(1)}) fusion(f32[]{:T(128)} %bitcast.74, bf16[1536,256]{1,0:T(8,128)(2,1)} %get-tuple-element.625, s32[]{:T(128)S(6)} %select_n.97, bf16[512,1792]{1,0:T(8,128)(2,1)} %get-tuple-element.624, s32[]{:T(128)S(6)} %select_n.95, pred[1536]{0:T(1024)(128)(4,1)S(1)} %get-tuple-element.631, ...), kind=kOutput, calls=%fused_computation.80.clone.1 | convolution fusion | flops 209976832 | bytes 3682312 | tf_op jit(solution)/shard_map/while/body/eval_jaxpr/dot_general | solution.py:74
  161.3 2.8 multiply_reduce_fusion.2
  169.9 3.3 %fusion.59 = (f32[512]{0:T(512)S(1)}, f32[512,1536]{1,0:T(8,128)S(1)}) fusion(f32[]{:T(128)} %bitcast.74, bf16[1536,256]{1,0:T(8,128)(2,1)} %get-tuple-element.625, s32[]{:T(128)S(6)} %select_n.97, bf16[512,1792]{1,0:T(8,128)(2,1)} %get-tuple-element.624, s32[]{:T(128)S(6)} %select_n.95, pred[1536]{0:T(1024)(128)(4,1)S(1)} %get-tuple-element.631, ...), kind=kOutput, calls=%fused_computation.80.clone.1 | convolution fusion | flops 209976832 | bytes 3682312 | tf_op jit(solution)/shard_map/while/body/eval_jaxpr/dot_general | solution.py:74
  174.6 2.8 multiply_reduce_fusion.2
  183.2 3.3 %fusion.59 = (f32[512]{0:T(512)S(1)}, f32[512,1536]{1,0:T(8,128)S(1)}) fusion(f32[]{:T(128)} %bitcast.74, bf16[1536,256]{1,0:T(8,128)(2,1)} %get-tuple-element.625, s32[]{:T(128)S(6)} %select_n.97, bf16[512,1792]{1,0:T(8,128)(2,1)} %get-tuple-element.624, s32[]{:T(128)S(6)} %select_n.95, pred[1536]{0:T(1024)(128)(4,1)S(1)} %get-tuple-element.631, ...), kind=kOutput, calls=%fused_computation.80.clone.1 | convolution fusion | flops 209976832 | bytes 3682312 | tf_op jit(solution)/shard_map/while/body/eval_jaxpr/dot_general | solution.py:74
  187.8 2.8 multiply_reduce_fusion.2
  196.5 3.3 %fusion.59 = (f32[512]{0:T(512)S(1)}, f32[512,1536]{1,0:T(8,128)S(1)}) fusion(f32[]{:T(128)} %bitcast.74, bf16[1536,256]{1,0:T(8,128)(2,1)} %get-tuple-element.625, s32[]{:T(128)S(6)} %select_n.97, bf16[512,1792]{1,0:T(8,128)(2,1)} %get-tuple-element.624, s32[]{:T(128)S(6)} %select_n.95, pred[1536]{0:T(1024)(128)(4,1)S(1)} %get-tuple-element.631, ...), kind=kOutput, calls=%fused_computation.80.clone.1 | convolution fusion | flops 209976832 | bytes 3682312 | tf_op jit(solution)/shard_map/while/body/eval_jaxpr/dot_general | solution.py:74
  201.2 2.8 multiply_reduce_fusion.2
  209.8 3.3 %fusion.59 = (f32[512]{0:T(512)S(1)}, f32[512,1536]{1,0:T(8,128)S(1)}) fusion(f32[]{:T(128)} %bitcast.74, bf16[1536,256]{1,0:T(8,128)(2,1)} %get-tuple-element.625, s32[]{:T(128)S(6)} %select_n.97, bf16[512,1792]{1,0:T(8,128)(2,1)} %get-tuple-element.624, s32[]{:T(128)S(6)} %select_n.95, pred[1536]{0:T(1024)(128)(4,1)S(1)} %get-tuple-element.631, ...), kind=kOutput, calls=%fused_computation.80.clone.1 | convolution fusion | flops 209976832 | bytes 3682312 | tf_op jit(solution)/shard_map/while/body/eval_jaxpr/dot_general | solution.py:74
  214.5 2.8 multiply_reduce_fusion.2
  223.1 3.3 %fusion.59 = (f32[512]{0:T(512)S(1)}, f32[512,1536]{1,0:T(8,128)S(1)}) fusion(f32[]{:T(128)} %bitcast.74, bf16[1536,256]{1,0:T(8,128)(2,1)} %get-tuple-element.625, s32[]{:T(128)S(6)} %select_n.97, bf16[512,1792]{1,0:T(8,128)(2,1)} %get-tuple-element.624, s32[]{:T(128)S(6)} %select_n.95, pred[1536]{0:T(1024)(128)(4,1)S(1)} %get-tuple-element.631, ...), kind=kOutput, calls=%fused_computation.80.clone.1 | convolution fusion | flops 209976832 | bytes 3682312 | tf_op jit(solution)/shard_map/while/body/eval_jaxpr/dot_general | solution.py:74
  227.8 2.8 multiply_reduce_fusion.2
  236.5 3.3 %fusion.59 = (f32[512]{0:T(512)S(1)}, f32[512,1536]{1,0:T(8,128)S(1)}) fusion(f32[]{:T(128)} %bitcast.74, bf16[1536,256]{1,0:T(8,128)(2,1)} %get-tuple-element.625, s32[]{:T(128)S(6)} %select_n.97, bf16[512,1792]{1,0:T(8,128)(2,1)} %get-tuple-element.624, s32[]{:T(128)S(6)} %select_n.95, pred[1536]{0:T(1024)(128)(4,1)S(1)} %get-tuple-element.631, ...), kind=kOutput, calls=%fused_computation.80.clone.1 | convolution fusion | flops 209976832 | bytes 3682312 | tf_op jit(solution)/shard_map/while/body/eval_jaxpr/dot_general | solution.py:74
  241.1 2.8 multiply_reduce_fusion.2
  249.8 3.3 %fusion.59 = (f32[512]{0:T(512)S(1)}, f32[512,1536]{1,0:T(8,128)S(1)}) fusion(f32[]{:T(128)} %bitcast.74, bf16[1536,256]{1,0:T(8,128)(2,1)} %get-tuple-element.625, s32[]{:T(128)S(6)} %select_n.97, bf16[512,1792]{1,0:T(8,128)(2,1)} %get-tuple-element.624, s32[]{:T(128)S(6)} %select_n.95, pred[1536]{0:T(1024)(128)(4,1)S(1)} %get-tuple-element.631, ...), kind=kOutput, calls=%fused_computation.80.clone.1 | convolution fusion | flops 209976832 | bytes 3682312 | tf_op jit(solution)/shard_map/while/body/eval_jaxpr/dot_general | solution.py:74
  254.4 2.8 multiply_reduce_fusion.2
  263.1 3.3 %fusion.59 = (f32[512]{0:T(512)S(1)}, f32[512,1536]{1,0:T(8,128)S(1)}) fusion(f32[]{:T(128)} %bitcast.74, bf16[1536,256]{1,0:T(8,128)(2,1)} %get-tuple-element.625, s32[]{:T(128)S(6)} %select_n.97, bf16[512,1792]{1,0:T(8,128)(2,1)} %get-tuple-element.624, s32[]{:T(128)S(6)} %select_n.95, pred[1536]{0:T(1024)(128)(4,1)S(1)} %get-tuple-element.631, ...), kind=kOutput, calls=%fused_computation.80.clone.1 | convolution fusion | flops 209976832 | bytes 3682312 | tf_op jit(solution)/shard_map/while/body/eval_jaxpr/dot_general | solution.py:74
  267.8 2.8 multiply_reduce_fusion.2
  276.1 1.9 collective-permute-start.3
  278.1 2.1 collective-permute-start.2
  280.1 11.2 %collective-permute-done.3 = bf16[2,512,256]{2,1,0:T(8,128)(2,1)S(1)} collective-permute-done((bf16[2,512,256]{2,1,0:T(8,128)(2,1)S(1)}, bf16[2,512,256]{2,1,0:T(8,128)(2,1)S(1)}, u32[]{:S(2)}, u32[]{:S(2)}) %collective-permute-start.3) | collective-permute-done | bytes 524320 | tf_op jit(solution)/shard_map/ppermute | solution.py:21
  291.3 5.9 %collective-permute-done.2 = bf16[2,512,256]{2,1,0:T(8,128)(2,1)S(1)} collective-permute-done((bf16[2,512,256]{2,1,0:T(8,128)(2,1)S(1)}, bf16[2,512,256]{2,1,0:T(8,128)(2,1)S(1)}, u32[]{:S(2)}, u32[]{:S(2)}) %collective-permute-start.2) | collective-permute-done | bytes 524320 | tf_op jit(solution)/shard_map/ppermute | solution.py:21
  (230 shorter events, 104.8 us)
Async XLA Ops:
  13.8 5.7 %copy-start.1 = (bf16[1,512,256]{2,1,0:T(8,128)(2,1)S(1)}, bf16[1,512,256]{2,1,0:T(8,128)(2,1)}, u32[]{:S(2)}) copy-start(bf16[1,512,256]{2,1,0:T(8,128)(2,1)} %param.11) | copy-start | bytes 786436
  13.8 6.4 %copy-start.2 = (bf16[1,512,256]{2,1,0:T(8,128)(2,1)S(1)}, bf16[1,512,256]{2,1,0:T(8,128)(2,1)}, u32[]{:S(2)}) copy-start(bf16[1,512,256]{2,1,0:T(8,128)(2,1)} %param.12) | copy-start | bytes 786436
  13.8 13.7 %copy-start.4 = (s32[1,512]{1,0:T(1,128)S(1)}, s32[1,512]{1,0:T(1,128)}, u32[]{:S(2)}) copy-start(s32[1,512]{1,0:T(1,128)} %param.16) | copy-start | bytes 6148
  13.8 72.2 %all-to-all-start = ((bf16[8,1,512,224]{2,3,1,0:T(8,128)(2,1)}), bf16[8,1,512,224]{2,3,1,0:T(8,128)(2,1)S(1)}, u32[]{:S(2)}, u32[]{:S(2)}) async-start(bf16[8,1,512,224]{2,3,1,0:T(8,128)(2,1)} %bitcast_dynamic-update-slice_fusion), calls=%async_computation | async-start | bytes 3670016 | tf_op jit(solution)/shard_map/all_to_all | solution.py:14
  20.9 63.7 %collective-permute-start.1 = (bf16[2,512,256]{2,1,0:T(8,128)(2,1)}, bf16[2,512,256]{2,1,0:T(8,128)(2,1)S(1)}, u32[]{:S(2)}, u32[]{:S(2)}) collective-permute-start(bf16[2,512,256]{2,1,0:T(8,128)(2,1)} %constant_dynamic-update-slice_fusion), channel_id=1, source_target_pairs={{0,1},{1,2},{2,3},{3,4},{4,5},{5,6},{6,7},{8,9},{9,10},{10,11},{11... | collective-permute-start | bytes 1572872 | tf_op jit(solution)/shard_map/ppermute | solution.py:21
  24.2 60.4 %collective-permute-start = (bf16[2,512,256]{2,1,0:T(8,128)(2,1)}, bf16[2,512,256]{2,1,0:T(8,128)(2,1)S(1)}, u32[]{:S(2)}, u32[]{:S(2)}) collective-permute-start(bf16[2,512,256]{2,1,0:T(8,128)(2,1)} %constant_dynamic-update-slice_fusion), channel_id=1, source_target_pairs={{0,2},{1,3},{2,4},{3,5},{4,6},{5,7},{8,10},{9,11},{10,12},{11,13},... | collective-permute-start | bytes 1572872 | tf_op jit(solution)/shard_map/ppermute | solution.py:21
  88.3 1.5 copy-start.5
  93.7 1.4 copy-start.3
  99.8 1.6 copy-start
  106.9 1.4 copy-start.3
  113.0 1.6 copy-start
  120.2 1.4 copy-start.3
  126.3 1.6 copy-start
  133.4 1.4 copy-start.3
  139.6 1.6 copy-start
  146.7 1.4 copy-start.3
  152.8 1.6 copy-start
  160.0 1.4 copy-start.3
  166.1 1.6 copy-start
  173.2 1.4 copy-start.3
  179.3 1.6 copy-start
  186.5 1.4 copy-start.3
  192.6 1.6 copy-start
  199.8 1.4 copy-start.3
  205.9 1.6 copy-start
  213.1 1.4 copy-start.3
  219.2 1.6 copy-start
  226.4 1.4 copy-start.3
  232.5 1.6 copy-start
  239.7 1.4 copy-start.3
  245.9 1.6 copy-start
  253.1 1.4 copy-start.3
  259.2 1.6 copy-start
  266.4 1.4 copy-start.3
  272.5 1.6 copy-start
  276.1 15.3 %collective-permute-start.3 = (bf16[2,512,256]{2,1,0:T(8,128)(2,1)S(1)}, bf16[2,512,256]{2,1,0:T(8,128)(2,1)S(1)}, u32[]{:S(2)}, u32[]{:S(2)}) collective-permute-start(bf16[2,512,256]{2,1,0:T(8,128)(2,1)S(1)} %pad_maximum_fusion.3), channel_id=1, source_target_pairs={{2,0},{3,1},{4,2},{5,3},{6,4},{7,5},{10,8},{11,9},{12,10},{13,11},... | collective-permute-start | bytes 1572872 | tf_op jit(solution)/shard_map/ppermute | solution.py:21
  278.1 19.2 %collective-permute-start.2 = (bf16[2,512,256]{2,1,0:T(8,128)(2,1)S(1)}, bf16[2,512,256]{2,1,0:T(8,128)(2,1)S(1)}, u32[]{:S(2)}, u32[]{:S(2)}) collective-permute-start(bf16[2,512,256]{2,1,0:T(8,128)(2,1)S(1)} %pad_maximum_fusion.2), channel_id=1, source_target_pairs={{1,0},{2,1},{3,2},{4,3},{5,4},{6,5},{7,6},{9,8},{10,9},{11,10},{12... | collective-permute-start | bytes 1572872 | tf_op jit(solution)/shard_map/ppermute | solution.py:21
